TPU v7x, 32 devices: a whole 2x2x4 slice. The times are simulated.
32 devices in a mesh: expert: 8 (over z, core), tensor: 4 (over y, x).
Axes of the slice: x: 2, y: 2, z: 4, core: 2. Of those that a mesh axis runs over, the one named last changes fastest.
Arguments:
- residual_in: bfloat16 [1024, 3584], P('expert'), may hold values from -8 to 8
- head_outputs: bfloat16 [1024, 4096], P('expert', 'tensor'), may hold values from -6 to 6
- out_weight: bfloat16 [4096, 3584], P('tensor'), may hold values from -0.09375 to 0.09375
- gain_in: float32 [3584], replicated, may hold values from 0.25 to 1.75
- dense_gate: bfloat16 [3584, 2432], P(None, 'tensor'), may hold values from -0.09375 to 0.09375
- dense_up: bfloat16 [3584, 2432], P(None, 'tensor'), may hold values from -0.09375 to 0.09375
- dense_down: bfloat16 [2432, 3584], P('tensor'), may hold values from -0.125 to 0.125
- expert_ids: int32 [1024, 2], P('expert'), may hold values from 0 to 7, all different within a row
- route_weights: float32 [1024, 2], P('expert'), may hold values from 0.1 to 1
- gain_moe: float32 [3584], replicated, may hold values from 0.25 to 1.75
- expert_gate: bfloat16 [8, 3584, 2432], P('expert', None, 'tensor'), may hold values from -0.09375 to 0.09375
- expert_up: bfloat16 [8, 3584, 2432], P('expert', None, 'tensor'), may hold values from -0.09375 to 0.09375
- expert_down: bfloat16 [8, 2432, 3584], P('expert', 'tensor'), may hold values from -0.125 to 0.125
Outputs:
- layer_out: bfloat16 [1024, 3584], P('expert', 'tensor')
Inputs may be any that keep to these rules, and one draw needn't show every extreme that they name: `expert_ids`: each row names two different experts.
All inputs are finite; a program needn't handle non-finite values.
Results may differ from a plain program's by a relative error of at most 0.006.
Values may be sent and summed in bfloat16 or wider, within the bound.
No kernel may reach another device: no remote copies, remote signals or barrier semaphores. Data moves between devices by JAX's collectives and lax.ppermute only.
A program may use at most 64 MiB of HBM per device.

v0:
```python
import jax
import jax.numpy as jnp
from jax import lax
from jax.sharding import PartitionSpec as P

eps = 1e-05


def shards(
    residual_in,
    head_outputs,
    out_weight,
    gain_in,
    dense_gate,
    dense_up,
    dense_down,
    expert_ids,
    route_weights,
    gain_moe,
    expert_gate,
    expert_up,
    expert_down,
):
    tok_rows, model_width = residual_in.shape
    experts_count = lax.axis_size("expert")
    tensor_count = lax.axis_size("tensor")
    capacity = 2 * tok_rows // experts_count
    slot_count = experts_count * capacity
    local_cols = model_width // tensor_count
    col_start = lax.axis_index("tensor") * local_cols
    x_float = residual_in.astype(jnp.float32)
    normed = (
        x_float * lax.rsqrt(jnp.mean(x_float * x_float, axis=1, keepdims=True) + eps) * gain_in
    ).astype(jnp.bfloat16)
    dense_hidden = (
        jax.nn.silu(jnp.dot(normed, dense_gate, preferred_element_type=jnp.float32))
        * jnp.dot(normed, dense_up, preferred_element_type=jnp.float32)
    ).astype(jnp.bfloat16)
    partial_value = jnp.dot(head_outputs, out_weight, preferred_element_type=jnp.float32) + jnp.dot(
        dense_hidden, dense_down, preferred_element_type=jnp.float32
    )
    flat_ids = expert_ids.reshape(-1)
    onehot = (flat_ids[:, None] == jnp.arange(experts_count, dtype=jnp.int32)[None, :]).astype(
        jnp.int32
    )
    earlier = jnp.cumsum(onehot, axis=0) - onehot
    position = jnp.sum(earlier * onehot, axis=1)
    slot_index = jnp.where(position < capacity, flat_ids * capacity + position, -1).reshape(
        tok_rows, 2
    )
    matches = slot_index[:, :, None] == jnp.arange(slot_count, dtype=jnp.int32)[None, None, :]
    placing = jnp.sum(matches.astype(jnp.bfloat16), axis=1)
    weighing = jnp.sum(matches.astype(jnp.float32) * route_weights[:, :, None], axis=1)
    shares = lax.psum_scatter(partial_value, "tensor", scatter_dimension=1, tiled=True)
    mixed_cols = lax.dynamic_slice_in_dim(x_float, col_start, local_cols, 1) + shares
    squares = lax.psum(jnp.sum(mixed_cols * mixed_cols, axis=1), "tensor")
    gain_cols = lax.dynamic_slice_in_dim(gain_moe, col_start, local_cols, 0)
    routed_cols = (mixed_cols * lax.rsqrt(squares / model_width + eps)[:, None] * gain_cols).astype(
        jnp.bfloat16
    )
    outgoing = lax.dot_general(
        placing, routed_cols, (((0,), (0,)), ((), ())), preferred_element_type=jnp.float32
    ).astype(jnp.bfloat16)
    received = lax.all_to_all(outgoing, "expert", split_axis=0, concat_axis=0, tiled=True)
    pieces = lax.all_gather(received, "tensor", axis=1, tiled=True)
    gate_rows = expert_gate[0]
    up_rows = expert_up[0]
    gate_sum = jnp.dot(pieces, gate_rows, preferred_element_type=jnp.float32)
    up_sum = jnp.dot(pieces, up_rows, preferred_element_type=jnp.float32)
    hidden = (jax.nn.silu(gate_sum) * up_sum).astype(jnp.bfloat16)
    expert_part = jnp.dot(hidden, expert_down[0], preferred_element_type=jnp.float32)
    expert_cols = lax.psum_scatter(
        expert_part.astype(jnp.bfloat16), "tensor", scatter_dimension=1, tiled=True
    )
    returned = lax.all_to_all(expert_cols, "expert", split_axis=0, concat_axis=0, tiled=True)
    moe_out = jnp.dot(weighing, returned.astype(jnp.float32), precision=lax.Precision.HIGHEST)
    return (mixed_cols + moe_out).astype(jnp.bfloat16)


def solution(mesh):
    return jax.shard_map(
        shards,
        mesh=mesh,
        in_specs=(
            P("expert", None),
            P("expert", "tensor"),
            P("tensor", None),
            P(),
            P(None, "tensor"),
            P(None, "tensor"),
            P("tensor", None),
            P("expert", None),
            P("expert", None),
            P(),
            P("expert", None, "tensor"),
            P("expert", None, "tensor"),
            P("expert", "tensor", None),
        ),
        out_specs=P("expert", "tensor"),
        check_vma=False,
    )
```

profile of v0, /device:TPU:0, one launch (start us, length us, event | category | flops | bytes accessed | tf_op | source)
XLA Modules:
  0.0 195.3 jit_solution(13092806147728898816)
XLA Ops:
  6.5 1.6 multiply_reduce_fusion
  8.2 4.3 %fusion.35 = f32[128,3584]{1,0:T(8,128)S(1)} fusion(bf16[128,1024]{1,0:T(8,128)(2,1)S(1)} %copy-done, bf16[1024,3584]{1,0:T(8,128)(2,1)} %param.15), kind=kOutput, calls=%fused_computation.49 | convolution fusion | flops 939524096 | bytes 9437184 | tf_op jit(solution)/shard_map/dot_general | solution.py:39
  12.5 1.4 fusion.25
  13.9 8.4 %convolution_add_fusion = f32[128,3584]{1,0:T(8,128)} fusion(f32[128,3584]{1,0:T(8,128)S(1)} %fusion.35, bf16[608,3584]{1,0:T(8,128)(2,1)} %param.19, bf16[3584,608]{0,1:T(8,128)(2,1)} %param.18, f32[128,608]{0,1:T(8,128)S(1)} %fusion.25, f32[3584]{0:T(1024)S(1)} %copy-done.2, f32[128]{0:T(128)S(1)} %add_rsqrt_fusion.1, bf16[128,3584]{1,0:T(8,128)(2,1)S(1)} %copy-done.1), kind=kOutput, calls=%fused_computation.1 | convolution fusion | flops 1118445568 | bytes 13629952 | tf_op jit(solution)/shard_map/dot_general | solution.py:39
  22.4 1.4 convert_element_type.38
  24.0 0.1 eq.38
  24.2 0.6 reduce-window.6
  24.8 0.2 slice_reduce_fusion
  25.1 0.1 reduce_sum.52
  25.5 0.8 dynamic_slice.7
  26.4 31.8 %reduce-scatter.5.cloned.1.call-done = f32[128,896]{1,0:T(8,128)} async-done(((f32[128,3584]{1,0:T(8,128)}), f32[128,896]{1,0:T(8,128)}) %reduce-scatter.5.cloned.1.call-update) | async-done | bytes 458768 | tf_op jit(solution)/shard_map/reduce_scatter | solution.py:54
  58.2 1.3 multiply_reduce_fusion.1
  59.5 8.9 %psum.7 = f32[128]{0:T(128)S(1)} all-reduce(f32[128]{0:T(128)S(1)} %get-tuple-element.5), channel_id=1, replica_groups=mesh['expert'=8,'tensor'=4] {'tensor'}, use_global_device_ids=true, to_apply=%region_8.9 | all-reduce | flops 128 | bytes 1024 | tf_op jit(solution)/shard_map/psum | solution.py:56
  68.4 0.3 convolution_convert_fusion.1
  68.8 18.4 %all_to_all.24 = bf16[8,32,896]{2,1,0:T(8,128)(2,1)} all-to-all(bf16[8,32,896]{2,1,0:T(8,128)(2,1)S(1)} %bitcast.43), channel_id=1, replica_groups=mesh['expert'=8,'tensor'=4] {'expert'}, dimensions={0} | all-to-all | bytes 917504 | tf_op jit(solution)/shard_map/all_to_all | solution.py:64
  87.3 31.1 %all-gather.2.cloned.1.call-done = bf16[256,3584]{1,0:T(8,128)(2,1)} async-done(((bf16[256,896]{1,0:T(8,128)(2,1)}), bf16[256,3584]{1,0:T(8,128)(2,1)}) %all-gather.2.cloned.1.call-update) | async-done | bytes 1835024 | tf_op jit(solution)/shard_map/all_gather | solution.py:65
  118.4 4.1 %fusion.3 = f32[256,608]{0,1:T(8,128)S(1)} fusion(bf16[256,3584]{1,0:T(8,128)(2,1)} %all-gather.2.cloned.1.call-done, bf16[1,3584,608]{1,2,0:T(8,128)(2,1)} %param.23), kind=kOutput, calls=%fused_computation.5 | convolution fusion | flops 1115684864 | bytes 6815744 | tf_op jit(solution)/shard_map/dot_general | solution.py:68
  122.5 9.2 %convolution_convert_fusion = bf16[256,3584]{1,0:T(8,128)(2,1)S(1)} fusion(bf16[1,608,3584]{2,1,0:T(8,128)(2,1)} %param.25, bf16[256,3584]{1,0:T(8,128)(2,1)} %all-gather.2.cloned.1.call-done, bf16[1,3584,608]{1,2,0:T(8,128)(2,1)} %param.24, f32[256,608]{0,1:T(8,128)S(1)} %fusion.3), kind=kOutput, calls=%fused_computation | convolution fusion | flops 2233221120 | bytes 13008896 | tf_op jit(solution)/shard_map/dot_general | solution.py:71
  131.7 2.3 %copy.31 = bf16[256,3584]{0,1:T(8,128)(2,1)} copy(bf16[256,3584]{1,0:T(8,128)(2,1)S(1)} %convolution_convert_fusion) | data formatting | bytes 3670016
  134.0 33.2 %reduce-scatter.7.cloned.1.call-done = bf16[896,256]{1,0:T(8,128)(2,1)} async-done(((bf16[3584,256]{1,0:T(8,128)(2,1)}), bf16[896,256]{1,0:T(8,128)(2,1)}) %reduce-scatter.7.cloned.1.call-update) | async-done | bytes 458768
  167.2 2.0 %copy.32 = bf16[256,896]{1,0:T(8,128)(2,1)} copy(bf16[256,896]{0,1:T(8,128)(2,1)} %bitcast.45) | data formatting | bytes 917504
  169.2 4.6 %all-to-all-start.1 = ((bf16[8,32,896]{2,1,0:T(8,128)(2,1)}), bf16[8,32,896]{2,1,0:T(8,128)(2,1)S(1)}, u32[]{:S(2)}, u32[]{:S(2)}) async-start(bf16[8,32,896]{2,1,0:T(8,128)(2,1)} %bitcast.7), calls=%async_computation.2 | async-start | bytes 917504 | tf_op jit(solution)/shard_map/all_to_all | solution.py:75
  173.9 13.8 %all-to-all-done.1 = bf16[8,32,896]{2,1,0:T(8,128)(2,1)S(1)} async-done(((bf16[8,32,896]{2,1,0:T(8,128)(2,1)}), bf16[8,32,896]{2,1,0:T(8,128)(2,1)S(1)}, u32[]{:S(2)}, u32[]{:S(2)}) %all-to-all-start.1) | async-done | bytes 458784 | tf_op jit(solution)/shard_map/all_to_all | solution.py:75
  187.7 1.1 fusion.11
  (35 shorter events, 1.0 us)
Async XLA Ops:
  6.5 1.6 copy-start
  6.5 51.6 %reduce-scatter.5.cloned.1.call-start = ((), (), s32[]{:S(2)}) async-start(), calls=%async_computation.4 | async-start | bytes 2293760 | tf_op jit(solution)/shard_map/reduce_scatter | solution.py:54
  6.5 6.0 %slice-start = ((s8[4358144]{0:T(1024)(128)(4,1)}), s8[4194304]{0:T(1024)(128)(4,1)S(1)}, s32[]{:S(2)}) async-start(s8[4358144]{0:T(1024)(128)(4,1)} %bitcast.40), calls=%async_computation.7 | async-start | bytes 8388608
  8.2 4.4 %copy-start.1 = (bf16[128,3584]{1,0:T(8,128)(2,1)S(1)}, bf16[128,3584]{1,0:T(8,128)(2,1)}, u32[]{:S(2)}) copy-start(bf16[128,3584]{1,0:T(8,128)(2,1)} %param.13) | copy-start | bytes 2752516
  8.2 4.4 %slice-start.1 = ((s8[4358144]{0:T(1024)(128)(4,1)}), s8[163840]{0:T(1024)(128)(4,1)S(1)}, s32[]{:S(2)}) async-start(s8[4358144]{0:T(1024)(128)(4,1)} %bitcast.40), calls=%async_computation.8 | async-start | bytes 327680
  8.2 4.4 %copy-start.2 = (f32[3584]{0:T(1024)S(1)}, f32[3584]{0:T(1024)}, u32[]{:S(2)}) copy-start(f32[3584]{0:T(1024)} %param.16) | copy-start | bytes 43012
  22.3 1.5 copy-start.3
  22.3 96.1 %all-gather.2.cloned.1.call-start = ((), (), s32[]{:S(2)}) async-start(), calls=%async_computation.5 | async-start | bytes 2293760 | tf_op jit(solution)/shard_map/all_gather | solution.py:65
  87.2 79.9 %reduce-scatter.7.cloned.1.call-start = ((), (), s32[]{:S(2)}) async-start(), calls=%async_computation.6 | async-start | bytes 2293760
  131.7 42.1 %copy-start.4 = (f32[128,2]{0,1:T(2,128)S(1)}, f32[128,2]{0,1:T(2,128)}, u32[]{:S(2)}) copy-start(f32[128,2]{0,1:T(2,128)} %param.21) | copy-start | bytes 3076
  169.2 18.5 %all-to-all-start.1 = ((bf16[8,32,896]{2,1,0:T(8,128)(2,1)}), bf16[8,32,896]{2,1,0:T(8,128)(2,1)S(1)}, u32[]{:S(2)}, u32[]{:S(2)}) async-start(bf16[8,32,896]{2,1,0:T(8,128)(2,1)} %bitcast.7), calls=%async_computation.2 | async-start | bytes 917504 | tf_op jit(solution)/shard_map/all_to_all | solution.py:75
Sparse Core Ops, SparseCore 0:
  22.4 35.7 reduce-scatter.4
  87.4 30.9 all-gather.1
  134.1 33.0 reduce-scatter.6
where the time goes:
time: 196 us; the launch traced here: 195 us
  waiting for transfers between devices  110 us (56%)
  matrix products  28.8 us (15%)
  blocking collectives  27.4 us (14%)
  between operations  13.3 us (7%)
  local copies, waits for them, and re-layouts  6.05 us (3%)
  other arithmetic  5.28 us (3%)
  starting transfers between devices  4.68 us (2%)
    unnamed x4, waiting for transfers between devices  33.2 us
    reduce_scatter x1, waiting for transfers between devices, shards(): lax.psum_scatter(partial_value, 'tensor', scatter_dimension=1, tiled=True)  31.8 us
    all_gather x1, waiting for transfers between devices, shards(): pieces = lax.all_gather(received, 'tensor', axis=1, tiled=True)  31.1 us
    all_to_all x1, blocking collectives, shards(): lax.all_to_all(outgoing, 'expert', split_axis=0, concat_axis=0, tiled=True)  18.4 us
    all_to_all x1, waiting for transfers between devices, shards(): lax.all_to_all(expert_cols, 'expert', split_axis=0, concat_axis=0, tiled=...  13.8 us
    dot_general x1, matrix products, shards(): jnp.dot(hidden, expert_down[0], preferred_element_type=jnp.float32)  9.19 us
    psum x1, blocking collectives, shards(): squares = lax.psum(jnp.sum(mixed_cols * mixed_cols, axis=1), 'tensor')  8.92 us
    dot_general x1, matrix products, shards(): jnp.dot(dense_hidden, dense_down, preferred_element_type=jnp.float32)  8.37 us
  transfers between devices with their start and end apart: 4, of which 4 were waited for; matrix products, arithmetic and copies ran while one was open for 2% of the time, Pallas kernels for 0%

commit v1 on v0

--- a/solution.py
+++ b/solution.py
@@ -62,7 +62,25 @@
         placing, routed_cols, (((0,), (0,)), ((), ())), preferred_element_type=jnp.float32
     ).astype(jnp.bfloat16)
     received = lax.all_to_all(outgoing, "expert", split_axis=0, concat_axis=0, tiled=True)
-    pieces = lax.all_gather(received, "tensor", axis=1, tiled=True)
+    length, here, rows = (lax.axis_size("tensor"), lax.axis_index("tensor"), received.shape[1])
+    right = [(i, (i + 1) % length) for i in range(length)]
+    left = [(i, (i - 1) % length) for i in range(length)]
+    pieces = jnp.zeros(
+        (*received.shape[:1], length * rows, *received.shape[1 + 1 :]), received.dtype
+    )
+    pieces = lax.dynamic_update_slice_in_dim(pieces, received, here * rows, axis=1)
+    from_left = from_right = received
+    middle = length // 2
+    for step in range(1, middle + 1):
+        from_left = lax.ppermute(from_left, "tensor", right)
+        pieces = lax.dynamic_update_slice_in_dim(
+            pieces, from_left, (here - step) % length * rows, axis=1
+        )
+        if step < length - middle:
+            from_right = lax.ppermute(from_right, "tensor", left)
+            pieces = lax.dynamic_update_slice_in_dim(
+                pieces, from_right, (here + step) % length * rows, axis=1
+            )
     gate_rows = expert_gate[0]
     up_rows = expert_up[0]
     gate_sum = jnp.dot(pieces, gate_rows, preferred_element_type=jnp.float32)

time: 196 us -> 196 us (level)
  waiting for transfers between devices: 110 us -> 107 us
  starting transfers between devices: 4.68 us -> 7.58 us
  local copies, waits for them, and re-layouts: 6.05 us -> 8.05 us
    all_gather x1 -> x0, waiting for transfers between devices: 31.1 us -> none  [shards(): pieces = lax.all_gather(received, 'tensor', axis=1, tiled=True)]
    ppermute x0 -> x3, waiting for transfers between devices: none -> 29.3 us  [the longest x2 19.7 us: shards(): from_left = lax.ppermute(from_left, 'tensor', right)]
    ppermute x0 -> x3, starting transfers between devices: none -> 2.93 us  [the longest x1 2.35 us: shards(): from_right = lax.ppermute(from_right, 'tensor', left)]
    unnamed x17 -> x19, local copies, waits for them, and re-layouts: 4.45 us -> 6.13 us
    unnamed x4 -> x3, waiting for transfers between devices: 33.2 us -> 31.7 us
  transfers between devices with their start and end apart: 4 -> 6, of which waited for: 4 -> 6; matrix products, arithmetic and copies ran while one was open for 2% -> 2% of each run, Pallas kernels for 0% -> 0%
where the time goes in v1:
time: 196 us
  waiting for transfers between devices  107 us (55%)
  matrix products  28.2 us (14%)
  blocking collectives  27.3 us (14%)
  between operations  13.6 us (7%)
  local copies, waits for them, and re-layouts  8.05 us (4%)
  starting transfers between devices  7.58 us (4%)
  other arithmetic  3.91 us (2%)
    reduce_scatter x1, waiting for transfers between devices, shards(): lax.psum_scatter(partial_value, 'tensor', scatter_dimension=1, tiled=True)  32.7 us
    unnamed x3, waiting for transfers between devices  31.7 us
    ppermute x2, waiting for transfers between devices, shards(): from_left = lax.ppermute(from_left, 'tensor', right)  19.7 us
    all_to_all x1, blocking collectives, shards(): lax.all_to_all(outgoing, 'expert', split_axis=0, concat_axis=0, tiled=True)  18.3 us
    all_to_all x1, waiting for transfers between devices, shards(): lax.all_to_all(expert_cols, 'expert', split_axis=0, concat_axis=0, tiled=...  13.8 us
    ppermute x1, waiting for transfers between devices, shards(): from_right = lax.ppermute(from_right, 'tensor', left)  9.57 us
    dot_general x1, matrix products, shards(): jnp.dot(hidden, expert_down[0], preferred_element_type=jnp.float32)  9.2 us
    psum x1, blocking collectives, shards(): squares = lax.psum(jnp.sum(mixed_cols * mixed_cols, axis=1), 'tensor')  8.94 us
  transfers between devices with their start and end apart: 6, of which 6 were waited for; matrix products, arithmetic and copies ran while one was open for 2% of the time, Pallas kernels for 0%

profile of v1, /device:TPU:0, one launch (start us, length us, event | category | flops | bytes accessed | tf_op | source)
XLA Modules:
  0.0 196.0 jit_solution(208001470419990178)
XLA Ops:
  6.5 1.6 multiply_reduce_fusion
  8.2 4.3 %fusion.28 = f32[128,3584]{1,0:T(8,128)S(1)} fusion(bf16[128,1024]{1,0:T(8,128)(2,1)S(1)} %copy-done, bf16[1024,3584]{1,0:T(8,128)(2,1)} %param.15), kind=kOutput, calls=%fused_computation.49 | convolution fusion | flops 939524096 | bytes 9437184 | tf_op jit(solution)/shard_map/dot_general | solution.py:39
  12.5 1.4 fusion.18
  13.9 8.4 %convolution_add_fusion = f32[128,3584]{1,0:T(8,128)} fusion(f32[128,3584]{1,0:T(8,128)S(1)} %fusion.28, bf16[608,3584]{1,0:T(8,128)(2,1)} %param.19, bf16[3584,608]{0,1:T(8,128)(2,1)} %param.18, f32[128,608]{0,1:T(8,128)S(1)} %fusion.18, f32[3584]{0:T(1024)S(1)} %copy-done.3, f32[128]{0:T(128)S(1)} %add_rsqrt_fusion.1, bf16[128,3584]{1,0:T(8,128)(2,1)S(1)} %copy-done.1), kind=kOutput, calls=%fused_computation.1 | convolution fusion | flops 1118445568 | bytes 13629952 | tf_op jit(solution)/shard_map/dot_general | solution.py:39
  23.4 0.6 reduce-window.6
  24.7 0.8 dynamic_slice.7
  25.6 32.7 %reduce-scatter.5.cloned.1.call-done = f32[128,896]{1,0:T(8,128)} async-done(((f32[128,3584]{1,0:T(8,128)}), f32[128,896]{1,0:T(8,128)}) %reduce-scatter.5.cloned.1.call-update) | async-done | bytes 458768 | tf_op jit(solution)/shard_map/reduce_scatter | solution.py:54
  58.2 1.2 multiply_reduce_fusion.1
  59.4 8.9 %psum.7 = f32[128]{0:T(128)S(1)} all-reduce(f32[128]{0:T(128)S(1)} %get-tuple-element.5), channel_id=1, replica_groups=mesh['expert'=8,'tensor'=4] {'tensor'}, use_global_device_ids=true, to_apply=%region_8.9 | all-reduce | flops 128 | bytes 1024 | tf_op jit(solution)/shard_map/psum | solution.py:56
  68.7 18.3 %all_to_all.24 = bf16[8,32,896]{2,1,0:T(8,128)(2,1)S(1)} all-to-all(bf16[8,32,896]{2,1,0:T(8,128)(2,1)S(1)} %bitcast.43), channel_id=1, replica_groups=mesh['expert'=8,'tensor'=4] {'expert'}, dimensions={0} | all-to-all | bytes 917504 | tf_op jit(solution)/shard_map/all_to_all | solution.py:64
  87.0 0.6 collective-permute-start
  87.6 2.4 %collective-permute-start.1 = (bf16[256,896]{1,0:T(8,128)(2,1)S(1)}, bf16[256,896]{1,0:T(8,128)(2,1)S(1)}, u32[]{:S(2)}, u32[]{:S(2)}) collective-permute-start(bf16[256,896]{1,0:T(8,128)(2,1)S(1)} %bitcast.41), channel_id=1, source_target_pairs={{0,3},{1,0},{2,1},{3,2},{4,7},{5,4},{6,5},{7,6},{8,11},{9,8},{10,9... | collective-permute-start | bytes 1376264 | tf_op jit(solution)/shard_map/ppermute | solution.py:80
  90.0 11.4 %collective-permute-done = bf16[256,896]{1,0:T(8,128)(2,1)S(1)} collective-permute-done((bf16[256,896]{1,0:T(8,128)(2,1)S(1)}, bf16[256,896]{1,0:T(8,128)(2,1)S(1)}, u32[]{:S(2)}, u32[]{:S(2)}) %collective-permute-start) | collective-permute-done | bytes 458784 | tf_op jit(solution)/shard_map/ppermute | solution.py:75
  101.6 9.6 %collective-permute-done.1 = bf16[256,896]{1,0:T(8,128)(2,1)S(1)} collective-permute-done((bf16[256,896]{1,0:T(8,128)(2,1)S(1)}, bf16[256,896]{1,0:T(8,128)(2,1)S(1)}, u32[]{:S(2)}, u32[]{:S(2)}) %collective-permute-start.1) | collective-permute-done | bytes 458784 | tf_op jit(solution)/shard_map/ppermute | solution.py:80
  111.2 8.4 %collective-permute-done.2 = bf16[256,896]{1,0:T(8,128)(2,1)S(1)} collective-permute-done((bf16[256,896]{1,0:T(8,128)(2,1)S(1)}, bf16[256,896]{1,0:T(8,128)(2,1)S(1)}, u32[]{:S(2)}, u32[]{:S(2)}) %collective-permute-start.2) | collective-permute-done | bytes 458784 | tf_op jit(solution)/shard_map/ppermute | solution.py:75
  119.6 1.2 copy-done.2
  120.9 3.5 %fusion.1 = f32[256,608]{0,1:T(8,128)S(1)} fusion(bf16[256,3584]{1,0:T(8,128)(2,1)S(1)} %constant_dynamic-update-slice_fusion, bf16[1,3584,608]{1,2,0:T(8,128)(2,1)} %param.24), kind=kOutput, calls=%fused_computation.3 | convolution fusion | flops 1115684864 | bytes 6815744 | tf_op jit(solution)/shard_map/dot_general | solution.py:87
  124.4 9.2 %convolution_convert_fusion = bf16[256,3584]{1,0:T(8,128)(2,1)S(1)} fusion(bf16[1,608,3584]{2,1,0:T(8,128)(2,1)} %param.25, f32[256,608]{0,1:T(8,128)S(1)} %fusion.1, bf16[256,3584]{1,0:T(8,128)(2,1)} %copy-done.2, bf16[1,3584,608]{1,2,0:T(8,128)(2,1)} %param.23), kind=kOutput, calls=%fused_computation | convolution fusion | flops 2233221120 | bytes 13008896 | tf_op jit(solution)/shard_map/dot_general | solution.py:89
  133.6 2.3 %copy.31 = bf16[256,3584]{0,1:T(8,128)(2,1)} copy(bf16[256,3584]{1,0:T(8,128)(2,1)S(1)} %convolution_convert_fusion) | data formatting | bytes 3670016
  136.0 31.6 %reduce-scatter.7.cloned.1.call-done = bf16[896,256]{1,0:T(8,128)(2,1)} async-done(((bf16[3584,256]{1,0:T(8,128)(2,1)}), bf16[896,256]{1,0:T(8,128)(2,1)}) %reduce-scatter.7.cloned.1.call-update) | async-done | bytes 458768
  167.6 2.0 %copy.32 = bf16[256,896]{1,0:T(8,128)(2,1)} copy(bf16[256,896]{0,1:T(8,128)(2,1)} %bitcast.45) | data formatting | bytes 917504
  169.6 4.6 %all-to-all-start.1 = ((bf16[8,32,896]{2,1,0:T(8,128)(2,1)}), bf16[8,32,896]{2,1,0:T(8,128)(2,1)S(1)}, u32[]{:S(2)}, u32[]{:S(2)}) async-start(bf16[8,32,896]{2,1,0:T(8,128)(2,1)} %bitcast.7), calls=%async_computation.2 | async-start | bytes 917504 | tf_op jit(solution)/shard_map/all_to_all | solution.py:93
  174.4 13.8 %all-to-all-done.1 = bf16[8,32,896]{2,1,0:T(8,128)(2,1)S(1)} async-done(((bf16[8,32,896]{2,1,0:T(8,128)(2,1)}), bf16[8,32,896]{2,1,0:T(8,128)(2,1)S(1)}, u32[]{:S(2)}, u32[]{:S(2)}) %all-to-all-start.1) | async-done | bytes 458784 | tf_op jit(solution)/shard_map/all_to_all | solution.py:93
  188.1 1.1 fusion.5
  (45 shorter events, 2.7 us)
Async XLA Ops:
  6.5 1.6 copy-start
  6.5 51.7 %reduce-scatter.5.cloned.1.call-start = ((), (), s32[]{:S(2)}) async-start(), calls=%async_computation.4 | async-start | bytes 2293760 | tf_op jit(solution)/shard_map/reduce_scatter | solution.py:54
  6.5 6.0 %slice-start = ((s8[4358144]{0:T(1024)(128)(4,1)}), s8[4194304]{0:T(1024)(128)(4,1)S(1)}, s32[]{:S(2)}) async-start(s8[4358144]{0:T(1024)(128)(4,1)} %bitcast.38), calls=%async_computation.6 | async-start | bytes 8388608
  8.2 4.4 %copy-start.1 = (bf16[128,3584]{1,0:T(8,128)(2,1)S(1)}, bf16[128,3584]{1,0:T(8,128)(2,1)}, u32[]{:S(2)}) copy-start(bf16[128,3584]{1,0:T(8,128)(2,1)} %param.13) | copy-start | bytes 2752516
  8.2 4.4 %slice-start.1 = ((s8[4358144]{0:T(1024)(128)(4,1)}), s8[163840]{0:T(1024)(128)(4,1)S(1)}, s32[]{:S(2)}) async-start(s8[4358144]{0:T(1024)(128)(4,1)} %bitcast.38), calls=%async_computation.7 | async-start | bytes 327680
  8.2 4.4 %copy-start.3 = (f32[3584]{0:T(1024)S(1)}, f32[3584]{0:T(1024)}, u32[]{:S(2)}) copy-start(f32[3584]{0:T(1024)} %param.16) | copy-start | bytes 43012
  22.3 0.7 copy-start.4
  22.3 145.3 %reduce-scatter.7.cloned.1.call-start = ((), (), s32[]{:S(2)}) async-start(), calls=%async_computation.5 | async-start | bytes 2293760
  87.0 14.3 %collective-permute-start = (bf16[256,896]{1,0:T(8,128)(2,1)S(1)}, bf16[256,896]{1,0:T(8,128)(2,1)S(1)}, u32[]{:S(2)}, u32[]{:S(2)}) collective-permute-start(bf16[256,896]{1,0:T(8,128)(2,1)S(1)} %bitcast.40), channel_id=1, source_target_pairs={{0,1},{1,2},{2,3},{3,0},{4,5},{5,6},{6,7},{7,4},{8,9},{9,10},{10,1... | collective-permute-start | bytes 1376264 | tf_op jit(solution)/shard_map/ppermute | solution.py:75
  87.6 23.5 %collective-permute-start.1 = (bf16[256,896]{1,0:T(8,128)(2,1)S(1)}, bf16[256,896]{1,0:T(8,128)(2,1)S(1)}, u32[]{:S(2)}, u32[]{:S(2)}) collective-permute-start(bf16[256,896]{1,0:T(8,128)(2,1)S(1)} %bitcast.41), channel_id=1, source_target_pairs={{0,3},{1,0},{2,1},{3,2},{4,7},{5,4},{6,5},{7,6},{8,11},{9,8},{10,9... | collective-permute-start | bytes 1376264 | tf_op jit(solution)/shard_map/ppermute | solution.py:80
  101.3 18.3 %collective-permute-start.2 = (bf16[256,896]{1,0:T(8,128)(2,1)S(1)}, bf16[256,896]{1,0:T(8,128)(2,1)S(1)}, u32[]{:S(2)}, u32[]{:S(2)}) collective-permute-start(bf16[256,896]{1,0:T(8,128)(2,1)S(1)} %collective-permute-done), channel_id=1, source_target_pairs={{0,1},{1,2},{2,3},{3,0},{4,5},{5,6},{6,7},{7,4},{8,9},{9,10},{10,1... | collective-permute-start | bytes 1376264 | tf_op jit(solution)/shard_map/ppermute | solution.py:75
  119.6 1.3 copy-start.2
  136.0 38.3 %copy-start.5 = (f32[128,2]{0,1:T(2,128)S(1)}, f32[128,2]{0,1:T(2,128)}, u32[]{:S(2)}) copy-start(f32[128,2]{0,1:T(2,128)} %param.21) | copy-start | bytes 3076
  169.6 18.5 %all-to-all-start.1 = ((bf16[8,32,896]{2,1,0:T(8,128)(2,1)}), bf16[8,32,896]{2,1,0:T(8,128)(2,1)S(1)}, u32[]{:S(2)}, u32[]{:S(2)}) async-start(bf16[8,32,896]{2,1,0:T(8,128)(2,1)} %bitcast.7), calls=%async_computation.2 | async-start | bytes 917504 | tf_op jit(solution)/shard_map/all_to_all | solution.py:93
Sparse Core Ops, SparseCore 0:
  22.4 35.7 reduce-scatter.4
  136.1 31.4 reduce-scatter.6
